TPU v7x, 32 devices: a whole 2x2x4 slice. The times are simulated.
32 devices in a mesh: ctx: 16 (over z, y, core), head: 2 (over x).
Axes of the slice: x: 2, y: 2, z: 4, core: 2. Of those that a mesh axis runs over, the one named last changes fastest.
Arguments:
- queries: bfloat16 [2048, 8192], P('ctx', 'head'), may hold values from -5.5 to 5.5
- keys: bfloat16 [2048, 1024], P('ctx', 'head'), may hold values from -5.5 to 5.5
- values: bfloat16 [2048, 1024], P('ctx', 'head'), may hold values from -6 to 6
- feature_weights: bfloat16 [64, 128, 64], P('head'), may hold values from -1 to 1
Outputs:
- attn_error: float32 [2048, 8192], P('ctx', 'head')
- loss: float32 [], replicated
- grad_w: float32 [64, 128, 64], P('head')
All inputs are finite; a program needn't handle non-finite values.
Results may differ from a plain program's by a relative error of at most 0.004.
Values may be sent and summed in bfloat16 or wider, within the bound.
No kernel may reach another device: no remote copies, remote signals or barrier semaphores. Data moves between devices by JAX's collectives and lax.ppermute only.
A program may use at most 192 MiB of HBM per device.

v0:
```python
import math
import jax
import jax.numpy as jnp
from jax import lax
from jax.sharding import PartitionSpec as P

HEAD_SIZE = 128
QUERY_HEADS = 64
KEY_VALUE_HEADS = 8
FM = 64
WIN = 64
phi_scale = 0.00390625
big_negative = -1e30
highest = lax.Precision.HIGHEST


def swapped(value, axis, distance):
    mask = 2**distance
    pairs = [(source, source ^ mask) for source in range(lax.axis_size(axis))]
    return lax.ppermute(value, axis, pairs)


def carried_in(value, axis, combine, identity):
    devices, here = (lax.axis_size(axis), lax.axis_index(axis))
    everything = jax.tree.map(
        lambda part, kind: lax.all_gather(part.astype(kind), axis),
        value,
        (jnp.bfloat16, jnp.bfloat16),
    )
    start = jax.tree.map(
        lambda part, zero: jnp.broadcast_to(jnp.asarray(zero, part.dtype), part.shape),
        value,
        identity,
    )

    def carried_step(k, before):
        reached = k < here
        new = combine(
            before, jax.tree.map(lambda part, own: part[k].astype(own.dtype), everything, value)
        )
        return jax.tree.map(lambda a, b: jnp.where(reached, a, b), new, before)

    return lax.fori_loop(0, devices, carried_step, start)


def prefix(value, axis, combine, identity):
    devices, here = (lax.axis_size(axis), lax.axis_index(axis))
    everything = jax.tree.map(
        lambda part, kind: lax.all_gather(part.astype(kind), axis),
        value,
        jax.tree.map(lambda a: jnp.bfloat16 if a.dtype == jnp.float32 else a.dtype, value),
    )
    start = jax.tree.map(
        lambda part, zero: jnp.broadcast_to(jnp.asarray(zero, part.dtype), part.shape),
        value,
        identity,
    )

    def prefix_step(k, before):
        at = devices - 1 - k
        reached = at > here
        new = combine(
            before, jax.tree.map(lambda part, own: part[at].astype(own.dtype), everything, value)
        )
        return jax.tree.map(lambda a, b: jnp.where(reached, a, b), new, before)

    return lax.fori_loop(0, devices, prefix_step, start)


def features(projection):
    return phi_scale * jnp.concatenate(
        [1.0 + jax.nn.elu(projection), 1.0 + jax.nn.elu(-projection)], axis=-1
    )


def feature_back(projection, grad_phi):
    half = projection.shape[-1]
    slope_plus = jnp.where(projection > 0, 1.0, jnp.exp(jnp.minimum(projection, 0.0)))
    slope_minus = jnp.where(projection < 0, 1.0, jnp.exp(jnp.minimum(-projection, 0.0)))
    return phi_scale * (grad_phi[..., :half] * slope_plus - grad_phi[..., half:] * slope_minus)


def add_pair(earlier, later):
    return (earlier[0] + later[0], earlier[1] + later[1])


def split_product(form, phi_part, data):
    upper = phi_part.astype(jnp.bfloat16)
    lower = (phi_part - upper.astype(jnp.float32)).astype(jnp.bfloat16)
    return jnp.einsum(form, upper, data, preferred_element_type=jnp.float32) + jnp.einsum(
        form, lower, data, preferred_element_type=jnp.float32
    )


def visit_partner(rows):
    for bit_index in range(lax.axis_size("ctx").bit_length() - 1):
        rows = swapped(rows, "ctx", bit_index)
    return rows


def return_partner(rows):
    for bit_index in range(lax.axis_size("ctx").bit_length() - 1):
        rows = swapped(rows.astype(jnp.bfloat16), "ctx", bit_index).astype(rows.dtype)
    return rows


def teacher_part(part, query_set, pos_set, key_block, value_block, key_pos, masked):
    scale_factor = 1.0 / math.sqrt(query_set.shape[-1])
    scores = (
        jnp.einsum("qgrd,kgd->grqk", query_set, key_block, preferred_element_type=jnp.float32)
        * scale_factor
    )
    if masked:
        causal = key_pos[None, :] <= pos_set[:, None]
        top = jnp.maximum(part[0], jnp.max(jnp.where(causal, scores, big_negative), axis=-1))
        weights = jnp.exp(jnp.where(causal, scores - top[..., None], big_negative))
    else:
        top = jnp.maximum(part[0], jnp.max(scores, axis=-1))
        weights = jnp.exp(scores - top[..., None])
    rescale = jnp.exp(part[0] - top)
    total = part[1] * rescale + jnp.sum(weights, axis=-1)
    mixed = part[2] * rescale[..., None] + jnp.einsum(
        "grqk,kgd->grqd",
        weights.astype(jnp.bfloat16),
        value_block,
        preferred_element_type=jnp.float32,
    )
    return (top, total, mixed)


def advance(part, row_set, key_block, value_block, key_pos, first):
    query_set, pos_set = row_set
    needed = first <= pos_set[-1]
    straddle = key_pos[-1] > pos_set[0]
    branch_index = jnp.where(needed, jnp.where(straddle, 2, 1), 0).astype(jnp.int32)
    return lax.switch(
        branch_index,
        [
            lambda current: current,
            lambda current: teacher_part(
                current, query_set, pos_set, key_block, value_block, key_pos, False
            ),
            lambda current: teacher_part(
                current, query_set, pos_set, key_block, value_block, key_pos, True
            ),
        ],
        part,
    )


def shards(queries, keys, values, feature_weights):
    local_rows = queries.shape[0]
    half_rows = local_rows // 2
    groups = keys.shape[1] // HEAD_SIZE
    group_ratio = QUERY_HEADS // KEY_VALUE_HEADS
    heads_here = groups * group_ratio
    ctx_count = lax.axis_size("ctx")
    ctx_place = lax.axis_index("ctx")
    own_start = ctx_place * local_rows
    query4 = queries.reshape(local_rows, groups, group_ratio, HEAD_SIZE)
    own_keys = keys.reshape(local_rows, groups, HEAD_SIZE)
    own_values = values.reshape(local_rows, groups, HEAD_SIZE)
    weight4 = feature_weights.reshape(groups, group_ratio, HEAD_SIZE, FM)
    scale = 1.0 / math.sqrt(HEAD_SIZE)
    query_pos = own_start + jnp.arange(local_rows, dtype=jnp.int32)
    tail_offsets = jnp.arange(WIN, dtype=jnp.int32)
    proj_own = jnp.einsum("kgd,grdf->grkf", own_keys, weight4, preferred_element_type=jnp.float32)
    first_set = (query4[:half_rows], query_pos[:half_rows])
    partner_start = (ctx_count - 1 - ctx_place) * local_rows
    visiting = visit_partner(query4[half_rows:])
    second_set = (visiting, partner_start + half_rows + jnp.arange(half_rows, dtype=jnp.int32))
    row_sets = (first_set, second_set)

    def add_tail(tails, key_block, value_block, key_pos):
        pick = (key_pos[None, :] == own_start - WIN + tail_offsets[:, None]).astype(jnp.bfloat16)
        return (
            tails[0]
            + jnp.einsum("wk,kgd->wgd", pick, key_block, preferred_element_type=jnp.float32),
            tails[1]
            + jnp.einsum("wk,kgd->wgd", pick, value_block, preferred_element_type=jnp.float32),
        )

    part_zero = (
        jnp.full((groups, group_ratio, half_rows), big_negative, jnp.float32),
        jnp.zeros((groups, group_ratio, half_rows), jnp.float32),
        jnp.zeros((groups, group_ratio, half_rows, HEAD_SIZE), jnp.float32),
    )
    tail_zero = (
        jnp.zeros((WIN, groups, HEAD_SIZE), jnp.float32),
        jnp.zeros((WIN, groups, HEAD_SIZE), jnp.float32),
    )
    state_zero = (
        jnp.zeros((groups, group_ratio, 2 * FM, HEAD_SIZE), jnp.float32),
        jnp.zeros((groups, group_ratio, 2 * FM), jnp.float32),
    )
    carry = ((part_zero, part_zero), tail_zero, ())
    key_piece = lax.all_gather(keys, "ctx", axis=0, tiled=True)
    value_piece = lax.all_gather(values, "ctx", axis=0, tiled=True)
    piece_rows = key_piece.shape[0]
    stride = math.gcd(piece_rows, local_rows)
    count = piece_rows // stride
    key_blocks = key_piece.reshape(count, stride, groups, HEAD_SIZE)
    value_blocks = value_piece.reshape(count, stride, groups, HEAD_SIZE)

    def fold_step(state, inputs):
        key_block, value_block, number = inputs
        first = number * stride
        key_pos = first + jnp.arange(stride, dtype=jnp.int32)
        parts_now, tails_now, states_now = state
        new_parts = (
            advance(parts_now[0], row_sets[0], key_block, value_block, key_pos, first),
            advance(parts_now[1], row_sets[1], key_block, value_block, key_pos, first),
        )
        earlier_block = first < own_start
        new_tails = lax.cond(
            earlier_block,
            lambda current: add_tail(current, key_block, value_block, key_pos),
            lambda current: current,
            tails_now,
        )
        return ((new_parts, new_tails, states_now), None)

    carry, unused = lax.scan(
        fold_step, carry, (key_blocks, value_blocks, jnp.arange(count, dtype=jnp.int32))
    )
    phi_own = features(proj_own)
    local_kv = split_product("grkf,kgd->grfd", phi_own, own_values)
    state_kv, state_norm = carried_in(
        (local_kv, jnp.sum(phi_own, axis=2)), "ctx", add_pair, state_zero
    )
    parts_done, tails_done = (carry[0], carry[1])
    teacher_first = parts_done[0][2] / parts_done[0][1][..., None]
    teacher_second = parts_done[1][2] / parts_done[1][1][..., None]
    teacher_second = return_partner(teacher_second)
    teacher = jnp.concatenate([teacher_first, teacher_second], axis=2)
    tail_key = tails_done[0].astype(jnp.bfloat16)
    tail_value = tails_done[1].astype(jnp.bfloat16)
    slab_key = jnp.concatenate([tail_key, own_keys], axis=0)
    slab_value = jnp.concatenate([tail_value, own_values], axis=0).astype(jnp.float32)
    slab_rows = WIN + local_rows
    slab_pos = own_start - WIN + jnp.arange(slab_rows, dtype=jnp.int32)
    is_tail = jnp.arange(slab_rows, dtype=jnp.int32) < WIN
    proj_tail = jnp.einsum("kgd,grdf->grkf", tail_key, weight4, preferred_element_type=jnp.float32)
    proj_slab = jnp.concatenate([proj_tail, proj_own], axis=2)
    phi_slab = features(proj_slab)
    proj_query = jnp.einsum("qgrd,grdf->grqf", query4, weight4, preferred_element_type=jnp.float32)
    phi_query = features(proj_query)
    scores = (
        jnp.einsum("qgrd,kgd->grqk", query4, slab_key, preferred_element_type=jnp.float32) * scale
    )
    window = (
        (slab_pos[None, :] >= query_pos[:, None] - WIN)
        & (slab_pos[None, :] <= query_pos[:, None])
        & (slab_pos[None, :] >= 0)
    )
    far = jnp.logical_not(is_tail)[None, :] & (slab_pos[None, :] < query_pos[:, None] - WIN)
    coefficient = far.astype(jnp.float32) - (window & is_tail[None, :]).astype(jnp.float32)
    window_top = jnp.max(jnp.where(window, scores, big_negative), axis=-1)
    local = jnp.exp(jnp.where(window, scores - window_top[..., None], big_negative))
    kernel = jnp.einsum("grqf,grkf->grqk", phi_query, phi_slab, precision=highest)
    mixed = local + coefficient * kernel
    numerator = jnp.einsum("grqk,kgd->grqd", mixed, slab_value, precision=highest) + jnp.einsum(
        "grqf,grfd->grqd", phi_query, state_kv, precision=highest
    )
    denominator = jnp.sum(mixed, axis=-1) + jnp.einsum(
        "grqf,grf->grq", phi_query, state_norm, precision=highest
    )
    student = numerator / denominator[..., None]
    error = student - teacher
    attn_error = jnp.transpose(error, (2, 0, 1, 3)).reshape(local_rows, heads_here * HEAD_SIZE)
    whole_rows = local_rows * ctx_count
    loss = lax.psum(jnp.sum(error * error), ("ctx", "head")) / (whole_rows * QUERY_HEADS)
    grad_out = 2.0 * error / denominator[..., None]
    grad_den = -jnp.sum(grad_out * student, axis=-1)
    later_kv = jnp.einsum("grqf,grqd->grfd", phi_query, grad_out, precision=highest)
    later_norm = jnp.einsum("grqf,grq->grf", phi_query, grad_den, precision=highest)
    suffix_kv, suffix_norm = prefix((later_kv, later_norm), "ctx", add_pair, state_zero)
    grad_lin = coefficient * (
        jnp.einsum("grqd,kgd->grqk", grad_out, slab_value, precision=highest) + grad_den[..., None]
    )
    grad_phi_query = (
        jnp.einsum("grqk,grkf->grqf", grad_lin, phi_slab, precision=highest)
        + jnp.einsum("grqd,grfd->grqf", grad_out, state_kv, precision=highest)
        + grad_den[..., None] * state_norm[:, :, None, :]
    )
    grad_phi_slab = jnp.einsum("grqk,grqf->grkf", grad_lin, phi_query, precision=highest)
    own_extra = (
        jnp.einsum("kgd,grfd->grkf", own_values.astype(jnp.float32), suffix_kv, precision=highest)
        + suffix_norm[:, :, None, :]
    )
    grad_phi_slab = grad_phi_slab + jnp.concatenate(
        [jnp.zeros((groups, group_ratio, WIN, 2 * FM), jnp.float32), own_extra], axis=2
    )
    grad_proj_query = feature_back(proj_query, grad_phi_query)
    grad_proj_slab = feature_back(proj_slab, grad_phi_slab)
    grad_local = jnp.einsum(
        "qgrd,grqf->grdf", query4.astype(jnp.float32), grad_proj_query, precision=highest
    ) + jnp.einsum(
        "kgd,grkf->grdf", slab_key.astype(jnp.float32), grad_proj_slab, precision=highest
    )
    grad_w = lax.psum(grad_local.reshape(heads_here, HEAD_SIZE, FM), "ctx")
    return (attn_error, loss, grad_w)


def solution(mesh):
    placed = (P("ctx", "head"), P("ctx", "head"), P("ctx", "head"), P("head", None, None))
    return jax.shard_map(
        shards,
        mesh=mesh,
        in_specs=placed,
        out_specs=(P("ctx", "head"), P(), P("head", None, None)),
        check_vma=False,
    )
```

profile of v0, /device:TPU:0, one launch (start us, length us, event | category | flops | bytes accessed | tf_op | source)
XLA Modules:
  0.0 783.3 jit_solution(9861084651910707477)
XLA Ops:
  25.6 4.3 fusion.116
  29.9 8.6 %collective-permute-done.1 = bf16[64,4,8,128]{3,2,1,0:T(8,128)(2,1)} collective-permute-done((bf16[64,4,8,128]{3,2,1,0:T(8,128)(2,1)}, bf16[64,4,8,128]{3,2,1,0:T(8,128)(2,1)}, u32[]{:S(2)}, u32[]{:S(2)}) %collective-permute-start.1) | collective-permute-done | bytes 524320 | tf_op jit(solution)/shard_map/ppermute | solution.py:20
  40.3 5.5 fusion.79
  45.8 13.8 %collective-permute-done.2 = bf16[64,4,8,128]{3,2,1,0:T(8,128)(2,1)} collective-permute-done((bf16[64,4,8,128]{3,2,1,0:T(8,128)(2,1)}, bf16[64,4,8,128]{3,2,1,0:T(8,128)(2,1)}, u32[]{:S(2)}, u32[]{:S(2)}) %collective-permute-start.2) | collective-permute-done | bytes 524320 | tf_op jit(solution)/shard_map/ppermute | solution.py:20
  64.5 4.3 maximum_multiply_fusion.1
  68.9 20.4 %collective-permute-done.3 = bf16[64,4,8,128]{3,2,1,0:T(8,128)(2,1)} collective-permute-done((bf16[64,4,8,128]{3,2,1,0:T(8,128)(2,1)}, bf16[64,4,8,128]{3,2,1,0:T(8,128)(2,1)}, u32[]{:S(2)}, u32[]{:S(2)}) %collective-permute-start.3) | collective-permute-done | bytes 524320 | tf_op jit(solution)/shard_map/ppermute | solution.py:20
  91.4 4.4 reshape.276
  95.8 16.4 %all-gather.11.cloned.1.call-done = bf16[2048,512]{1,0:T(8,128)(2,1)} async-done(((bf16[128,512]{1,0:T(8,128)(2,1)}), bf16[2048,512]{1,0:T(8,128)(2,1)}) %all-gather.11.cloned.1.call-update) | async-done | bytes 2097168 | tf_op jit(solution)/shard_map/all_gather | solution.py:198
  112.2 4.0 reshape.277
  118.3 193.6 %while.59 = (s32[]{:T(128)}, f32[4,8,64]{2,1,0:T(8,128)S(1)}, f32[4,8,64]{2,1,0:T(8,128)S(1)}, f32[4,8,64,128]{3,2,1,0:T(8,128)S(1)}, f32[4,8,64]{2,1,0:T(8,128)...) while((s32[]{:T(128)}, f32[4,8,64]{2,1,0:T(8,128)S(1)}, ...), condition=%wide.region_17.18_spmd.clone, body=%wide.region_0.17_spmd.clone.sunk | while | flops 291086528 | bytes 14226523 | solution.py:223
  316.5 64.0 %all-gather.1 = bf16[64,8,128]{2,1,0:T(8,128)(2,1)} all-gather(bf16[4,8,128]{2,1,0:T(8,128)(2,1)S(1)} %fusion.143), channel_id=3, replica_groups=mesh['ctx'=16,'head'=2] {'ctx'}, dimensions={0}, use_global_device_ids=true | all-gather | bytes 139264 | tf_op jit(solution)/shard_map/all_gather | solution.py:26
  384.5 4.6 fusion.46
  389.1 4.7 fusion.109
  393.8 4.8 collective-permute-done.5
  400.9 11.1 %collective-permute-done.6 = bf16[4,8,64,128]{3,2,1,0:T(8,128)(2,1)S(1)} collective-permute-done((bf16[4,8,64,128]{3,2,1,0:T(8,128)(2,1)S(1)}, bf16[4,8,64,128]{3,2,1,0:T(8,128)(2,1)S(1)}, u32[]{:S(2)}, u32[]{:S(2)}) %collective-permute-start.6) | collective-permute-done | bytes 524320 | tf_op jit(solution)/shard_map/ppermute | solution.py:20
  413.3 5.2 fusion.122
  418.5 18.1 %collective-permute-done.7 = bf16[4,8,64,128]{3,2,1,0:T(8,128)(2,1)S(1)} collective-permute-done((bf16[4,8,64,128]{3,2,1,0:T(8,128)(2,1)S(1)}, bf16[4,8,64,128]{3,2,1,0:T(8,128)(2,1)S(1)}, u32[]{:S(2)}, u32[]{:S(2)}) %collective-permute-start.7) | collective-permute-done | bytes 524320 | tf_op jit(solution)/shard_map/ppermute | solution.py:20
  437.7 49.1 %while.60 = (s32[]{:T(128)}, f32[4,8,128,128]{3,2,1,0:T(8,128)S(1)}, f32[4,8,128]{2,1,0:T(8,128)S(1)}, s32[]{:T(128)}, bf16[16,4,8,128,128]{4,3,2,1,0:T(8,128)(2...) while((s32[]{:T(128)}, f32[4,8,128,128]{3,2,1,0:T(8,128)S(1)}, ...), condition=%wide.region_21.22_spmd.clone, body=%wide.region_20.21_spmd.clone.sunk | while | flops 2113540 | bytes 5283955 | solution.py:43
  486.7 5.7 fusion.150
  492.5 6.4 multiply_reduce_fusion
  500.2 4.6 convolution_convert_fusion
  505.4 3.6 fusion.151
  509.0 19.1 %all-gather.3 = bf16[64,8,128]{2,1,0:T(8,128)(2,1)S(1)} all-gather(bf16[4,8,128]{2,1,0:T(8,128)(2,1)S(1)} %convert_element_type.142), channel_id=5, replica_groups=mesh['ctx'=16,'head'=2] {'ctx'}, dimensions={0}, use_global_device_ids=true | all-gather | bytes 139264 | tf_op jit(solution)/shard_map/all_gather | solution.py:49
  531.3 7.9 %fusion.68 = f32[4,8,128,128]{3,2,1,0:T(8,128)S(1)} fusion(f32[4,8,128,192]{2,3,1,0:T(8,128)S(1)} %fusion.121, f32[4,8,128]{2,1,0:T(8,128)S(1)} %neg.21, f32[128,192]{0,1:T(8,128)S(1)} %convert_subtract_fusion, f32[4,8,192,64]{3,2,1,0:T(8,128)S(1)} %copy-done.11, f32[4,8,192,64]{3,2,1,0:T(8,128)S(1)} %copy-done.9), kind=kOutput, calls=%fused_computation.116 | convolution fusion | flops 1211105280 | bytes 8503296 | tf_op jit(solution)/shard_map/grqk,grkf->grqf/dot_general | solution.py:282
  539.2 4.8 multiply_add_fusion.4
  544.1 4.5 fusion.83
  548.6 81.4 %all-gather.15.cloned.1.call-done = bf16[64,8,128,128]{3,2,1,0:T(8,128)(2,1)} async-done(((bf16[4,8,128,128]{3,2,1,0:T(8,128)(2,1)}), bf16[64,8,128,128]{3,2,1,0:T(8,128)(2,1)}) %all-gather.15.cloned.1.call-update) | async-done | bytes 16777232 | tf_op jit(solution)/shard_map/all_gather | solution.py:49
  630.0 38.6 %while.61 = (s32[]{:T(128)}, f32[4,8,128,128]{3,2,1,0:T(8,128)S(1)}, f32[4,8,128]{2,1,0:T(8,128)S(1)}, s32[]{:T(128)}, bf16[16,4,8,128,128]{4,3,2,1,0:T(8,128)(2...) while((s32[]{:T(128)}, ...), condition=%wide.region_27.28_spmd.clone, body=%wide.region_26.27_spmd.clone.sunk | while | flops 2113544 | bytes 5284017 | solution.py:67
  670.2 5.7 pad_add_fusion
  675.9 5.3 fusion.102
  681.2 39.0 %psum.14 = f32[]{:T(128)} all-reduce(f32[]{:T(128)} %get-tuple-element.673), channel_id=1, replica_groups=mesh['ctx'=16,'head'=2] {'ctx','head'}, use_global_device_ids=true, to_apply=%region_24.25 | all-reduce | flops 1 | bytes 8 | tf_op jit(solution)/shard_map/psum | solution.py:272
  724.6 48.3 %all-reduce.3.cloned.1.call-done = f32[32,128,64]{1,2,0:T(8,128)} async-done(((f32[32,128,64]{1,2,0:T(8,128)}), f32[32,128,64]{1,2,0:T(8,128)}) %all-reduce.3.cloned.1.call-update) | async-done | bytes 1048592 | tf_op jit(solution)/shard_map/psum | solution.py:301
  (483 shorter events, 321.2 us)
Async XLA Ops:
  7.2 84.2 %all-gather.9.cloned.1.call-start = ((), (), s32[]{:S(2)}) async-start(), calls=%async_computation | async-start | bytes 2228224 | tf_op jit(solution)/shard_map/all_gather | solution.py:197
  7.9 104.2 %all-gather.11.cloned.1.call-start = ((), (), s32[]{:S(2)}) async-start(), calls=%async_computation.1 | async-start | bytes 2228224 | tf_op jit(solution)/shard_map/all_gather | solution.py:198
  8.7 429.0 %all-gather.13.cloned.1.call-start = ((), (), s32[]{:S(2)}) async-start(), calls=%async_computation.3 | async-start | bytes 17825792 | tf_op jit(solution)/shard_map/all_gather | solution.py:26
  10.8 53.0 %copy-start.22 = (bf16[128,512]{0,1:T(8,128)(2,1)}, bf16[128,512]{0,1:T(8,128)(2,1)S(1)}, u32[]{:S(2)}) copy-start(bf16[128,512]{0,1:T(8,128)(2,1)S(1)} %copy.138) | copy-start | bytes 393220
  17.9 612.1 %all-gather.15.cloned.1.call-start = ((), (), s32[]{:S(2)}) async-start(), calls=%async_computation.4 | async-start | bytes 17825792 | tf_op jit(solution)/shard_map/all_gather | solution.py:49
  20.1 2.9 collective-permute-start
  23.1 15.4 %collective-permute-start.1 = (bf16[64,4,8,128]{3,2,1,0:T(8,128)(2,1)}, bf16[64,4,8,128]{3,2,1,0:T(8,128)(2,1)}, u32[]{:S(2)}, u32[]{:S(2)}) collective-permute-start(bf16[64,4,8,128]{3,2,1,0:T(8,128)(2,1)} %collective-permute-done), channel_id=1, source_target_pairs={{0,4},{2,6},{4,0},{6,2},{8,12},{10,14},{12,8},{14,10},{16,20},{18,... | collective-permute-start | bytes 1572872 | tf_op jit(solution)/shard_map/ppermute | solution.py:20
  29.9 16.0 %copy-start.28 = (u8[4,128,64]{2,1,0:T(8,128)(4,1)}, u8[4,128,64]{2,1,0:T(8,128)(4,1)S(1)}, u32[]{:S(2)}) copy-start(u8[4,128,64]{2,1,0:T(8,128)(4,1)S(1)} %get-tuple-element.671) | copy-start | bytes 98308
  38.5 21.1 %collective-permute-start.2 = (bf16[64,4,8,128]{3,2,1,0:T(8,128)(2,1)}, bf16[64,4,8,128]{3,2,1,0:T(8,128)(2,1)}, u32[]{:S(2)}, u32[]{:S(2)}) collective-permute-start(bf16[64,4,8,128]{3,2,1,0:T(8,128)(2,1)} %collective-permute-done.1), channel_id=1, source_target_pairs={{0,8},{2,10},{4,12},{6,14},{8,0},{10,2},{12,4},{14,6},{16,24},{18,... | collective-permute-start | bytes 1572872 | tf_op jit(solution)/shard_map/ppermute | solution.py:20
  40.3 21.7 %copy-start.14 = (f32[4,8,128,64]{3,2,1,0:T(8,128)S(1)}, f32[4,8,128,64]{3,2,1,0:T(8,128)}, u32[]{:S(2)}) copy-start(f32[4,8,128,64]{3,2,1,0:T(8,128)} %copy-done.13) | copy-start | bytes 3145732
  59.6 29.8 %collective-permute-start.3 = (bf16[64,4,8,128]{3,2,1,0:T(8,128)(2,1)}, bf16[64,4,8,128]{3,2,1,0:T(8,128)(2,1)}, u32[]{:S(2)}, u32[]{:S(2)}) collective-permute-start(bf16[64,4,8,128]{3,2,1,0:T(8,128)(2,1)} %collective-permute-done.2), channel_id=1, source_target_pairs={{0,16},{2,18},{4,20},{6,22},{8,24},{10,26},{12,28},{14,30},{16,0},... | collective-permute-start | bytes 1572872 | tf_op jit(solution)/shard_map/ppermute | solution.py:20
  313.0 71.4 %collective-permute-start.4 = (bf16[4,8,64,128]{3,2,1,0:T(8,128)(2,1)}, bf16[4,8,64,128]{3,2,1,0:T(8,128)(2,1)S(1)}, u32[]{:S(2)}, u32[]{:S(2)}) collective-permute-start(bf16[4,8,64,128]{3,2,1,0:T(8,128)(2,1)} %divide_convert_fusion), channel_id=1, source_target_pairs={{0,2},{2,0},{4,6},{6,4},{8,10},{10,8},{12,14},{14,12},{16,18},{18,... | collective-permute-start | bytes 1572872 | tf_op jit(solution)/shard_map/ppermute | solution.py:20
  384.4 14.2 %collective-permute-start.5 = (bf16[4,8,64,128]{3,2,1,0:T(8,128)(2,1)S(1)}, bf16[4,8,64,128]{3,2,1,0:T(8,128)(2,1)S(1)}, u32[]{:S(2)}, u32[]{:S(2)}) collective-permute-start(bf16[4,8,64,128]{3,2,1,0:T(8,128)(2,1)S(1)} %collective-permute-done.4), channel_id=1, source_target_pairs={{0,4},{2,6},{4,0},{6,2},{8,12},{10,14},{12,8},{14,10},{16,20},{18,... | collective-permute-start | bytes 1572872 | tf_op jit(solution)/shard_map/ppermute | solution.py:20
  389.1 9.6 %copy-start.20 = (bf16[16,8,32,128]{3,2,1,0:T(8,128)(2,1)S(1)}, bf16[16,8,32,128]{3,2,1,0:T(8,128)(2,1)}, u32[]{:S(2)}) copy-start(bf16[16,8,32,128]{3,2,1,0:T(8,128)(2,1)} %copy.204) | copy-start | bytes 3145732
  389.1 9.6 %copy-start.27 = (bf16[128,4,128]{2,0,1:T(8,128)(2,1)S(1)}, bf16[128,4,128]{2,0,1:T(8,128)(2,1)}, u32[]{:S(2)}) copy-start(bf16[128,4,128]{2,0,1:T(8,128)(2,1)} %copy.128) | copy-start | bytes 393220
  393.8 5.5 copy-start.17
  398.6 13.4 %collective-permute-start.6 = (bf16[4,8,64,128]{3,2,1,0:T(8,128)(2,1)S(1)}, bf16[4,8,64,128]{3,2,1,0:T(8,128)(2,1)S(1)}, u32[]{:S(2)}, u32[]{:S(2)}) collective-permute-start(bf16[4,8,64,128]{3,2,1,0:T(8,128)(2,1)S(1)} %collective-permute-done.5), channel_id=1, source_target_pairs={{0,8},{2,10},{4,12},{6,14},{8,0},{10,2},{12,4},{14,6},{16,24},{18,... | collective-permute-start | bytes 1572872 | tf_op jit(solution)/shard_map/ppermute | solution.py:20
  400.9 12.4 %copy-start.26 = (bf16[128,4,128]{2,0,1:T(8,128)(2,1)S(1)}, bf16[128,4,128]{2,0,1:T(8,128)(2,1)}, u32[]{:S(2)}) copy-start(bf16[128,4,128]{2,0,1:T(8,128)(2,1)} %copy.139) | copy-start | bytes 393220
  412.0 24.6 %collective-permute-start.7 = (bf16[4,8,64,128]{3,2,1,0:T(8,128)(2,1)S(1)}, bf16[4,8,64,128]{3,2,1,0:T(8,128)(2,1)S(1)}, u32[]{:S(2)}, u32[]{:S(2)}) collective-permute-start(bf16[4,8,64,128]{3,2,1,0:T(8,128)(2,1)S(1)} %collective-permute-done.6), channel_id=1, source_target_pairs={{0,16},{2,18},{4,20},{6,22},{8,24},{10,26},{12,28},{14,30},{16,0},... | collective-permute-start | bytes 1572872 | tf_op jit(solution)/shard_map/ppermute | solution.py:20
  413.3 24.3 %copy-start.2 = (f32[4,8,128,128]{3,2,1,0:T(8,128)S(1)}, f32[4,8,128,128]{3,2,1,0:T(8,128)}, u32[]{:S(2)}) copy-start(f32[4,8,128,128]{3,2,1,0:T(8,128)} %custom-call) | copy-start | bytes 6291460
  486.7 12.1 %copy-start.3 = (f32[4,8,128,128]{3,2,1,0:T(8,128)}, f32[4,8,128,128]{3,2,1,0:T(8,128)S(1)}, u32[]{:S(2)}) copy-start(f32[4,8,128,128]{3,2,1,0:T(8,128)S(1)} %get-tuple-element.496) | copy-start | bytes 6291460
  486.7 5.8 copy-start.6
  504.8 268.1 %all-reduce.3.cloned.1.call-start = ((), (), s32[]{:S(2)}) async-start(), calls=%async_computation.2 | async-start | bytes 2097152 | tf_op jit(solution)/shard_map/psum | solution.py:301
  505.3 25.9 %copy-start.11 = (f32[4,8,192,64]{3,2,1,0:T(8,128)S(1)}, f32[4,8,192,64]{3,2,1,0:T(8,128)}, u32[]{:S(2)}) copy-start(f32[4,8,192,64]{3,2,1,0:T(8,128)} %copy-done.10) | copy-start | bytes 4718596
  531.3 7.9 %copy-start.12 = (f32[4,8,128,192]{2,3,1,0:T(8,128)}, f32[4,8,128,192]{2,3,1,0:T(8,128)S(1)}, u32[]{:S(2)}) copy-start(f32[4,8,128,192]{2,3,1,0:T(8,128)S(1)} %fusion.121) | copy-start | bytes 9437188
  531.3 7.9 %copy-start.4 = (f32[4,8,128,128]{3,2,1,0:T(8,128)S(1)}, f32[4,8,128,128]{3,2,1,0:T(8,128)}, u32[]{:S(2)}) copy-start(f32[4,8,128,128]{3,2,1,0:T(8,128)} %copy-done.3) | copy-start | bytes 6291460
  531.3 7.9 %copy-start.16 = (f32[4,8,128,128]{3,2,1,0:T(8,128)S(1)}, f32[4,8,128,128]{3,2,1,0:T(8,128)}, u32[]{:S(2)}) copy-start(f32[4,8,128,128]{3,2,1,0:T(8,128)} %copy-done.15) | copy-start | bytes 6291460
  630.0 38.6 %copy-start.23 = (bf16[128,512]{0,1:T(8,128)(2,1)S(1)}, bf16[128,512]{0,1:T(8,128)(2,1)}, u32[]{:S(2)}) copy-start(bf16[128,512]{0,1:T(8,128)(2,1)} %copy-done.22) | copy-start | bytes 393220
  670.2 5.7 copy-start.19
  670.2 5.8 copy-start.25
  670.2 5.8 copy-start.31
  722.1 53.1 %copy-start.1 = (bf16[32,128,64]{1,2,0:T(8,128)(2,1)S(1)}, bf16[32,128,64]{1,2,0:T(8,128)(2,1)}, u32[]{:S(2)}) copy-start(bf16[32,128,64]{1,2,0:T(8,128)(2,1)} %param.21) | copy-start | bytes 1572868
  (13 other events, 49.1 us)
Sparse Core Ops, SparseCore 0:
  10.2 45.6 all-gather.8
  58.0 54.1 all-gather.10
  114.3 125.7 all-gather.12
  505.0 124.9 all-gather.14
  681.3 91.5 all-reduce.2
where the time goes:
time: 796 us; the launch traced here: 783 us
  waiting for transfers between devices  224 us (28%)
  blocking collectives  122 us (15%)
  matrix products  120 us (15%)
  other arithmetic  120 us (15%)
  local copies, waits for them, and re-layouts  96.2 us (12%)
  loops' own time  72.7 us (9%)
  between operations  16.5 us (2%)
  starting transfers between devices  11 us (1%)
    all_gather x1, waiting for transfers between devices, prefix(): lax.all_gather(part.astype(kind), axis)  81.4 us
    ppermute x8, waiting for transfers between devices, swapped(): return lax.ppermute(value, axis, pairs)  76.8 us
    another operation x1, loops' own time, shards(): lax.scan(fold_step, carry, (key_blocks, value_blocks, jnp.arange(count, d...  70.5 us
    all_gather x1, blocking collectives, carried_in(): lax.all_gather(part.astype(kind), axis)  64 us
    select_n x32, other arithmetic, carried_step(): return jax.tree.map(lambda a, b: jnp.where(reached, a, b), new, before)  49 us
    psum x1, waiting for transfers between devices, shards(): grad_w = lax.psum(grad_local.reshape(heads_here, HEAD_SIZE, FM), 'ctx')  48.3 us
    psum x1, blocking collectives, shards(): lax.psum(jnp.sum(error * error), ('ctx', 'head'))  39 us
    dynamic_slice x64, local copies, waits for them, and re-layouts, shards(): lax.scan(fold_step, carry, (key_blocks, value_blocks, jnp.arange(count, d...  38.7 us
  transfers between devices with their start and end apart: 13, of which 9 were waited for; matrix products, arithmetic and copies ran while one was open for 28% of the time, Pallas kernels for 0%

commit v1 on v0

--- a/solution.py
+++ b/solution.py
@@ -12,6 +12,31 @@
 phi_scale = 0.00390625
 big_negative = -1e30
 highest = lax.Precision.HIGHEST
+
+
+def state_play(field, axis_no):
+    block_now = jax.lax.axis_size("ctx")
+    kept_arr = jax.lax.axis_index("ctx")
+    front, finding, y1 = (block_now, kept_arr, field.shape[axis_no])
+    sides = tuple((idx * front if num == axis_no else idx for num, idx in enumerate(field.shape)))
+    all_rows = lax.dynamic_update_slice_in_dim(
+        jnp.zeros(sides, field.dtype), field, finding * y1, axis=axis_no
+    )
+    z1 = part_now = field
+    for ii in tuple(range(1, front // 2 + 1)):
+        current_value = tuple(((num, (num + 1) % front) for num in range(front)))
+        z1 = jax.lax.ppermute(z1, "ctx", current_value)
+        all_rows = lax.dynamic_update_slice_in_dim(
+            all_rows, z1, (finding - ii) % front * y1, axis=axis_no
+        )
+        if 2 * ii < front:
+            part_now = jax.lax.ppermute(
+                part_now, "ctx", tuple(((num, (num - 1) % front) for num in range(front)))
+            )
+            all_rows = lax.dynamic_update_slice_in_dim(
+                all_rows, part_now, (finding + ii) % front * y1, axis=axis_no
+            )
+    return all_rows
 
 
 def swapped(value, axis, distance):
@@ -195,7 +220,7 @@
     )
     carry = ((part_zero, part_zero), tail_zero, ())
     key_piece = lax.all_gather(keys, "ctx", axis=0, tiled=True)
-    value_piece = lax.all_gather(values, "ctx", axis=0, tiled=True)
+    value_piece = state_play(values, 0)
     piece_rows = key_piece.shape[0]
     stride = math.gcd(piece_rows, local_rows)
     count = piece_rows // stride

time: 796 us -> 832 us (1.045)
  starting transfers between devices: 11 us -> 48 us
  local copies, waits for them, and re-layouts: 96.2 us -> 108 us
  waiting for transfers between devices: 224 us -> 213 us
  blocking collectives: 122 us -> 131 us
    ppermute x0 -> x15, waiting for transfers between devices: none -> 50.9 us  [the longest x8 38.1 us: state_play(): z1 = jax.lax.ppermute(z1, 'ctx', current_value)]
    ppermute x8, waiting for transfers between devices: 76.8 us -> 32.8 us  [swapped(): return lax.ppermute(value, axis, pairs)]
    ppermute x0 -> x15, starting transfers between devices: none -> 38.2 us  [the longest x7 30.4 us: state_play(): jax.lax.ppermute(part_now, 'ctx', tuple(((num, (num - 1) % front) for num...]
    all_gather x1 -> x0, waiting for transfers between devices: 16.4 us -> none  [shards(): value_piece = lax.all_gather(values, 'ctx', axis=0, tiled=True)]
    squeeze x0 -> x16, local copies, waits for them, and re-layouts: none -> 15.2 us  [shards(): lax.scan(fold_step, carry, (key_blocks, value_blocks, jnp.arange(count, d...]
    dynamic_slice x64 -> x32, local copies, waits for them, and re-layouts: 38.7 us -> 24.9 us  [shards(): lax.scan(fold_step, carry, (key_blocks, value_blocks, jnp.arange(count, d...]
    ppermute x0 -> x15, local copies, waits for them, and re-layouts: none -> 11.8 us  [the longest x8 6.42 us: state_play(): z1 = jax.lax.ppermute(z1, 'ctx', current_value)]
    unnamed x74 -> x88, local copies, waits for them, and re-layouts: 14.9 us -> 24.7 us
  transfers between devices with their start and end apart: 13 -> 27, of which waited for: 9 -> 17; matrix products, arithmetic and copies ran while one was open for 28% -> 27% of each run, Pallas kernels for 0% -> 0%
where the time goes in v1:
time: 832 us; the launch traced here: 818 us
  waiting for transfers between devices  213 us (26%)
  blocking collectives  131 us (16%)
  matrix products  118 us (14%)
  other arithmetic  114 us (14%)
  local copies, waits for them, and re-layouts  108 us (13%)
  loops' own time  70 us (8%)
  starting transfers between devices  48 us (6%)
  between operations  17.1 us (2%)
    all_gather x1, waiting for transfers between devices, prefix(): lax.all_gather(part.astype(kind), axis)  80.1 us
    all_gather x1, blocking collectives, carried_in(): lax.all_gather(part.astype(kind), axis)  72 us
    another operation x1, loops' own time, shards(): lax.scan(fold_step, carry, (key_blocks, value_blocks, jnp.arange(count, d...  67.6 us
    select_n x32, other arithmetic, carried_step(): return jax.tree.map(lambda a, b: jnp.where(reached, a, b), new, before)  49 us
    psum x1, waiting for transfers between devices, shards(): grad_w = lax.psum(grad_local.reshape(heads_here, HEAD_SIZE, FM), 'ctx')  48.3 us
    psum x1, blocking collectives, shards(): lax.psum(jnp.sum(error * error), ('ctx', 'head'))  38.9 us
    ppermute x8, waiting for transfers between devices, state_play(): z1 = jax.lax.ppermute(z1, 'ctx', current_value)  38.1 us
    select_n x32, other arithmetic, prefix_step(): return jax.tree.map(lambda a, b: jnp.where(reached, a, b), new, before)  38 us
  transfers between devices with their start and end apart: 27, of which 17 were waited for; matrix products, arithmetic and copies ran while one was open for 27% of the time, Pallas kernels for 0%

profile of v1, /device:TPU:0, one launch (start us, length us, event | category | flops | bytes accessed | tf_op | source)
XLA Modules:
  0.0 818.4 jit_solution(3640379099639403416)
XLA Ops:
  17.7 5.1 collective-permute-start.1
  52.0 4.5 collective-permute-start.5
  60.0 4.2 collective-permute-start.6
  75.1 4.7 collective-permute-start.9
  79.9 17.1 %collective-permute-done.8 = bf16[128,512]{1,0:T(8,128)(2,1)} collective-permute-done((bf16[128,512]{1,0:T(8,128)(2,1)}, bf16[128,512]{1,0:T(8,128)(2,1)}, u32[]{:S(2)}, u32[]{:S(2)}) %collective-permute-start.8) | collective-permute-done | bytes 131104 | tf_op jit(solution)/shard_map/ppermute | solution.py:28
  100.2 4.6 collective-permute-start.11
  111.1 4.8 collective-permute-start.13
  122.1 7.9 collective-permute-done.13
  130.1 5.6 collective-permute-done.14
  138.8 4.3 copy.184
  150.6 184.9 %while.59 = (s32[]{:T(128)}, f32[4,8,64]{2,1,0:T(8,128)S(1)}, f32[4,8,64]{2,1,0:T(8,128)S(1)}, f32[4,8,64,128]{3,2,1,0:T(8,128)S(1)}, f32[4,8,64]{2,1,0:T(8,128)...) while((s32[]{:T(128)}, f32[4,8,64]{2,1,0:T(8,128)S(1)}, ...), condition=%wide.region_17.18_spmd.clone, body=%wide.region_0.17_spmd.clone.sunk | while | flops 291086528 | bytes 13964383 | solution.py:248
  335.9 8.0 collective-permute-start.19
  343.9 72.0 %all-gather.1 = bf16[64,8,128]{2,1,0:T(8,128)(2,1)} all-gather(bf16[4,8,128]{2,1,0:T(8,128)(2,1)S(1)} %fusion.143), channel_id=3, replica_groups=mesh['ctx'=16,'head'=2] {'ctx'}, dimensions={0}, use_global_device_ids=true | all-gather | bytes 139264 | tf_op jit(solution)/shard_map/all_gather | solution.py:51
  421.5 4.4 fusion.46
  425.9 4.7 fusion.109
  436.6 11.0 %collective-permute-done.21 = bf16[4,8,64,128]{3,2,1,0:T(8,128)(2,1)S(1)} collective-permute-done((bf16[4,8,64,128]{3,2,1,0:T(8,128)(2,1)S(1)}, bf16[4,8,64,128]{3,2,1,0:T(8,128)(2,1)S(1)}, u32[]{:S(2)}, u32[]{:S(2)}) %collective-permute-start.21) | collective-permute-done | bytes 524320 | tf_op jit(solution)/shard_map/ppermute | solution.py:45
  449.0 5.2 fusion.122
  454.2 18.1 %collective-permute-done.22 = bf16[4,8,64,128]{3,2,1,0:T(8,128)(2,1)S(1)} collective-permute-done((bf16[4,8,64,128]{3,2,1,0:T(8,128)(2,1)S(1)}, bf16[4,8,64,128]{3,2,1,0:T(8,128)(2,1)S(1)}, u32[]{:S(2)}, u32[]{:S(2)}) %collective-permute-start.22) | collective-permute-done | bytes 524320 | tf_op jit(solution)/shard_map/ppermute | solution.py:45
  473.3 49.1 %while.60 = (s32[]{:T(128)}, f32[4,8,128,128]{3,2,1,0:T(8,128)S(1)}, f32[4,8,128]{2,1,0:T(8,128)S(1)}, s32[]{:T(128)}, bf16[16,4,8,128,128]{4,3,2,1,0:T(8,128)(2...) while((s32[]{:T(128)}, f32[4,8,128,128]{3,2,1,0:T(8,128)S(1)}, ...), condition=%wide.region_21.22_spmd.clone, body=%wide.region_20.21_spmd.clone.sunk | while | flops 2113540 | bytes 5283955 | solution.py:68
  522.4 5.7 fusion.150
  528.2 6.4 multiply_reduce_fusion
  535.8 4.6 convolution_convert_fusion
  544.6 20.0 %all-gather.3 = bf16[64,8,128]{2,1,0:T(8,128)(2,1)S(1)} all-gather(bf16[4,8,128]{2,1,0:T(8,128)(2,1)S(1)} %convert_element_type.142), channel_id=5, replica_groups=mesh['ctx'=16,'head'=2] {'ctx'}, dimensions={0}, use_global_device_ids=true | all-gather | bytes 139264 | tf_op jit(solution)/shard_map/all_gather | solution.py:74
  567.9 7.9 fusion.68
  575.8 4.8 multiply_add_fusion.4
  580.6 4.5 fusion.83
  585.2 80.1 %all-gather.12.cloned.1.call-done = bf16[64,8,128,128]{3,2,1,0:T(8,128)(2,1)} async-done(((bf16[4,8,128,128]{3,2,1,0:T(8,128)(2,1)}), bf16[64,8,128,128]{3,2,1,0:T(8,128)(2,1)}) %all-gather.12.cloned.1.call-update) | async-done | bytes 16777232 | tf_op jit(solution)/shard_map/all_gather | solution.py:74
  665.2 38.6 %while.61 = (s32[]{:T(128)}, f32[4,8,128,128]{3,2,1,0:T(8,128)S(1)}, f32[4,8,128]{2,1,0:T(8,128)S(1)}, s32[]{:T(128)}, bf16[16,4,8,128,128]{4,3,2,1,0:T(8,128)(2...) while((s32[]{:T(128)}, ...), condition=%wide.region_27.28_spmd.clone, body=%wide.region_26.27_spmd.clone.sunk | while | flops 2113544 | bytes 5284017 | solution.py:92
  705.4 5.7 pad_add_fusion
  711.2 5.3 fusion.102
  716.5 38.9 %psum.14 = f32[]{:T(128)} all-reduce(f32[]{:T(128)} %get-tuple-element.673), channel_id=1, replica_groups=mesh['ctx'=16,'head'=2] {'ctx','head'}, use_global_device_ids=true, to_apply=%region_24.25 | all-reduce | flops 1 | bytes 8 | tf_op jit(solution)/shard_map/psum | solution.py:297
  759.8 48.3 %all-reduce.3.cloned.1.call-done = f32[32,128,64]{1,2,0:T(8,128)} async-done(((f32[32,128,64]{1,2,0:T(8,128)}), f32[32,128,64]{1,2,0:T(8,128)}) %all-reduce.3.cloned.1.call-update) | async-done | bytes 1048592 | tf_op jit(solution)/shard_map/psum | solution.py:326
  (539 shorter events, 370.7 us)
Async XLA Ops:
  7.2 137.9 %all-gather.8.cloned.1.call-start = ((), (), s32[]{:S(2)}) async-start(), calls=%async_computation | async-start | bytes 2228224 | tf_op jit(solution)/shard_map/all_gather | solution.py:222
  7.9 465.4 %all-gather.10.cloned.1.call-start = ((), (), s32[]{:S(2)}) async-start(), calls=%async_computation.2 | async-start | bytes 17825792 | tf_op jit(solution)/shard_map/all_gather | solution.py:51
  10.0 29.1 %copy-start.20 = (bf16[128,512]{0,1:T(8,128)(2,1)}, bf16[128,512]{0,1:T(8,128)(2,1)S(1)}, u32[]{:S(2)}) copy-start(bf16[128,512]{0,1:T(8,128)(2,1)S(1)} %copy.167) | copy-start | bytes 393220
  17.1 648.1 %all-gather.12.cloned.1.call-start = ((), (), s32[]{:S(2)}) async-start(), calls=%async_computation.3 | async-start | bytes 17825792 | tf_op jit(solution)/shard_map/all_gather | solution.py:74
  17.2 22.7 %collective-permute-start = (bf16[128,512]{1,0:T(8,128)(2,1)}, bf16[128,512]{1,0:T(8,128)(2,1)}, u32[]{:S(2)}, u32[]{:S(2)}) collective-permute-start(bf16[128,512]{1,0:T(8,128)(2,1)} %param.20), channel_id=1, source_target_pairs={{0,2},{2,4},{4,6},{6,8},{8,10},{10,12},{12,14},{14,16},{16,18},{18... | collective-permute-start | bytes 393224 | tf_op jit(solution)/shard_map/ppermute | solution.py:28
  17.7 23.8 %collective-permute-start.1 = (bf16[128,512]{1,0:T(8,128)(2,1)}, bf16[128,512]{1,0:T(8,128)(2,1)}, u32[]{:S(2)}, u32[]{:S(2)}) collective-permute-start(bf16[128,512]{1,0:T(8,128)(2,1)} %param.20), channel_id=1, source_target_pairs={{0,30},{2,0},{4,2},{6,4},{8,6},{10,8},{12,10},{14,12},{16,14},{18,... | collective-permute-start | bytes 393224 | tf_op jit(solution)/shard_map/ppermute | solution.py:33
  25.7 15.7 %collective-permute-start.15 = (bf16[64,4,8,128]{3,2,1,0:T(8,128)(2,1)}, bf16[64,4,8,128]{3,2,1,0:T(8,128)(2,1)}, u32[]{:S(2)}, u32[]{:S(2)}) collective-permute-start(bf16[64,4,8,128]{3,2,1,0:T(8,128)(2,1)} %bitcast.101), channel_id=1, source_target_pairs={{0,2},{2,0},{4,6},{6,4},{8,10},{10,8},{12,14},{14,12},{16,18},{18,... | collective-permute-start | bytes 1572872 | tf_op jit(solution)/shard_map/ppermute | solution.py:45
  40.9 9.2 %collective-permute-start.2 = (bf16[128,512]{1,0:T(8,128)(2,1)}, bf16[128,512]{1,0:T(8,128)(2,1)S(1)}, u32[]{:S(2)}, u32[]{:S(2)}) collective-permute-start(bf16[128,512]{1,0:T(8,128)(2,1)} %collective-permute-done), channel_id=1, source_target_pairs={{0,2},{2,4},{4,6},{6,8},{8,10},{10,12},{12,14},{14,16},{16,18},{18... | collective-permute-start | bytes 393224 | tf_op jit(solution)/shard_map/ppermute | solution.py:28
  41.5 27.0 %collective-permute-start.16 = (bf16[64,4,8,128]{3,2,1,0:T(8,128)(2,1)}, bf16[64,4,8,128]{3,2,1,0:T(8,128)(2,1)}, u32[]{:S(2)}, u32[]{:S(2)}) collective-permute-start(bf16[64,4,8,128]{3,2,1,0:T(8,128)(2,1)} %collective-permute-done.15), channel_id=1, source_target_pairs={{0,4},{2,6},{4,0},{6,2},{8,12},{10,14},{12,8},{14,10},{16,20},{18,... | collective-permute-start | bytes 1572872 | tf_op jit(solution)/shard_map/ppermute | solution.py:45
  42.6 8.4 %collective-permute-start.3 = (bf16[128,512]{1,0:T(8,128)(2,1)}, bf16[128,512]{1,0:T(8,128)(2,1)}, u32[]{:S(2)}, u32[]{:S(2)}) collective-permute-start(bf16[128,512]{1,0:T(8,128)(2,1)} %collective-permute-done.1), channel_id=1, source_target_pairs={{0,30},{2,0},{4,2},{6,4},{8,6},{10,8},{12,10},{14,12},{16,14},{18,... | collective-permute-start | bytes 393224 | tf_op jit(solution)/shard_map/ppermute | solution.py:33
  50.8 9.0 %collective-permute-start.4 = (bf16[128,512]{1,0:T(8,128)(2,1)}, bf16[128,512]{1,0:T(8,128)(2,1)S(1)}, u32[]{:S(2)}, u32[]{:S(2)}) collective-permute-start(bf16[128,512]{1,0:T(8,128)(2,1)} %copy-done.32), channel_id=1, source_target_pairs={{0,2},{2,4},{4,6},{6,8},{8,10},{10,12},{12,14},{14,16},{16,18},{18... | collective-permute-start | bytes 393224 | tf_op jit(solution)/shard_map/ppermute | solution.py:28
  52.0 12.6 %collective-permute-start.5 = (bf16[128,512]{1,0:T(8,128)(2,1)}, bf16[128,512]{1,0:T(8,128)(2,1)}, u32[]{:S(2)}, u32[]{:S(2)}) collective-permute-start(bf16[128,512]{1,0:T(8,128)(2,1)} %collective-permute-done.3), channel_id=1, source_target_pairs={{0,30},{2,0},{4,2},{6,4},{8,6},{10,8},{12,10},{14,12},{16,14},{18,... | collective-permute-start | bytes 393224 | tf_op jit(solution)/shard_map/ppermute | solution.py:33
  60.0 9.6 %collective-permute-start.6 = (bf16[128,512]{1,0:T(8,128)(2,1)S(1)}, bf16[128,512]{1,0:T(8,128)(2,1)}, u32[]{:S(2)}, u32[]{:S(2)}) collective-permute-start(bf16[128,512]{1,0:T(8,128)(2,1)S(1)} %collective-permute-done.4), channel_id=1, source_target_pairs={{0,2},{2,4},{4,6},{6,8},{8,10},{10,12},{12,14},{14,16},{16,18},{18... | collective-permute-start | bytes 393224 | tf_op jit(solution)/shard_map/ppermute | solution.py:28
  65.6 8.5 %collective-permute-start.7 = (bf16[128,512]{1,0:T(8,128)(2,1)}, bf16[128,512]{1,0:T(8,128)(2,1)}, u32[]{:S(2)}, u32[]{:S(2)}) collective-permute-start(bf16[128,512]{1,0:T(8,128)(2,1)} %collective-permute-done.5), channel_id=1, source_target_pairs={{0,30},{2,0},{4,2},{6,4},{8,6},{10,8},{12,10},{14,12},{16,14},{18,... | collective-permute-start | bytes 393224 | tf_op jit(solution)/shard_map/ppermute | solution.py:33
  68.4 40.9 %collective-permute-start.17 = (bf16[64,4,8,128]{3,2,1,0:T(8,128)(2,1)}, bf16[64,4,8,128]{3,2,1,0:T(8,128)(2,1)}, u32[]{:S(2)}, u32[]{:S(2)}) collective-permute-start(bf16[64,4,8,128]{3,2,1,0:T(8,128)(2,1)} %collective-permute-done.16), channel_id=1, source_target_pairs={{0,8},{2,10},{4,12},{6,14},{8,0},{10,2},{12,4},{14,6},{16,24},{18,... | collective-permute-start | bytes 1572872 | tf_op jit(solution)/shard_map/ppermute | solution.py:45
  70.6 26.3 %collective-permute-start.8 = (bf16[128,512]{1,0:T(8,128)(2,1)}, bf16[128,512]{1,0:T(8,128)(2,1)}, u32[]{:S(2)}, u32[]{:S(2)}) collective-permute-start(bf16[128,512]{1,0:T(8,128)(2,1)} %collective-permute-done.6), channel_id=1, source_target_pairs={{0,2},{2,4},{4,6},{6,8},{8,10},{10,12},{12,14},{14,16},{16,18},{18... | collective-permute-start | bytes 393224 | tf_op jit(solution)/shard_map/ppermute | solution.py:28
  75.1 24.9 %collective-permute-start.9 = (bf16[128,512]{1,0:T(8,128)(2,1)}, bf16[128,512]{1,0:T(8,128)(2,1)S(1)}, u32[]{:S(2)}, u32[]{:S(2)}) collective-permute-start(bf16[128,512]{1,0:T(8,128)(2,1)} %collective-permute-done.7), channel_id=1, source_target_pairs={{0,30},{2,0},{4,2},{6,4},{8,6},{10,8},{12,10},{14,12},{16,14},{18,... | collective-permute-start | bytes 393224 | tf_op jit(solution)/shard_map/ppermute | solution.py:33
  98.0 10.3 %collective-permute-start.10 = (bf16[128,512]{1,0:T(8,128)(2,1)}, bf16[128,512]{1,0:T(8,128)(2,1)}, u32[]{:S(2)}, u32[]{:S(2)}) collective-permute-start(bf16[128,512]{1,0:T(8,128)(2,1)} %collective-permute-done.8), channel_id=1, source_target_pairs={{0,2},{2,4},{4,6},{6,8},{8,10},{10,12},{12,14},{14,16},{16,18},{18... | collective-permute-start | bytes 393224 | tf_op jit(solution)/shard_map/ppermute | solution.py:28
  100.2 9.9 %collective-permute-start.11 = (bf16[128,512]{1,0:T(8,128)(2,1)S(1)}, bf16[128,512]{1,0:T(8,128)(2,1)}, u32[]{:S(2)}, u32[]{:S(2)}) collective-permute-start(bf16[128,512]{1,0:T(8,128)(2,1)S(1)} %collective-permute-done.9), channel_id=1, source_target_pairs={{0,30},{2,0},{4,2},{6,4},{8,6},{10,8},{12,10},{14,12},{16,14},{18,... | collective-permute-start | bytes 393224 | tf_op jit(solution)/shard_map/ppermute | solution.py:33
  109.3 10.7 %collective-permute-start.12 = (bf16[128,512]{1,0:T(8,128)(2,1)}, bf16[128,512]{1,0:T(8,128)(2,1)}, u32[]{:S(2)}, u32[]{:S(2)}) collective-permute-start(bf16[128,512]{1,0:T(8,128)(2,1)} %collective-permute-done.10), channel_id=1, source_target_pairs={{0,2},{2,4},{4,6},{6,8},{8,10},{10,12},{12,14},{14,16},{16,18},{18... | collective-permute-start | bytes 393224 | tf_op jit(solution)/shard_map/ppermute | solution.py:28
  109.4 33.7 %collective-permute-start.18 = (bf16[64,4,8,128]{3,2,1,0:T(8,128)(2,1)}, bf16[64,4,8,128]{3,2,1,0:T(8,128)(2,1)}, u32[]{:S(2)}, u32[]{:S(2)}) collective-permute-start(bf16[64,4,8,128]{3,2,1,0:T(8,128)(2,1)} %collective-permute-done.17), channel_id=1, source_target_pairs={{0,16},{2,18},{4,20},{6,22},{8,24},{10,26},{12,28},{14,30},{16,0},... | collective-permute-start | bytes 1572872 | tf_op jit(solution)/shard_map/ppermute | solution.py:45
  111.1 18.9 %collective-permute-start.13 = (bf16[128,512]{1,0:T(8,128)(2,1)}, bf16[128,512]{1,0:T(8,128)(2,1)S(1)}, u32[]{:S(2)}, u32[]{:S(2)}) collective-permute-start(bf16[128,512]{1,0:T(8,128)(2,1)} %collective-permute-done.11), channel_id=1, source_target_pairs={{0,30},{2,0},{4,2},{6,4},{8,6},{10,8},{12,10},{14,12},{16,14},{18,... | collective-permute-start | bytes 393224 | tf_op jit(solution)/shard_map/ppermute | solution.py:33
  121.0 14.7 %collective-permute-start.14 = (bf16[128,512]{1,0:T(8,128)(2,1)}, bf16[128,512]{1,0:T(8,128)(2,1)}, u32[]{:S(2)}, u32[]{:S(2)}) collective-permute-start(bf16[128,512]{1,0:T(8,128)(2,1)} %collective-permute-done.12), channel_id=1, source_target_pairs={{0,2},{2,4},{4,6},{6,8},{8,10},{10,12},{12,14},{14,16},{16,18},{18... | collective-permute-start | bytes 393224 | tf_op jit(solution)/shard_map/ppermute | solution.py:28
  335.9 83.9 %collective-permute-start.19 = (bf16[4,8,64,128]{3,2,1,0:T(8,128)(2,1)S(1)}, bf16[4,8,64,128]{3,2,1,0:T(8,128)(2,1)}, u32[]{:S(2)}, u32[]{:S(2)}) collective-permute-start(bf16[4,8,64,128]{3,2,1,0:T(8,128)(2,1)S(1)} %divide_convert_fusion), channel_id=1, source_target_pairs={{0,2},{2,0},{4,6},{6,4},{8,10},{10,8},{12,14},{14,12},{16,18},{18,... | collective-permute-start | bytes 1572872 | tf_op jit(solution)/shard_map/ppermute | solution.py:45
  419.8 14.4 %collective-permute-start.20 = (bf16[4,8,64,128]{3,2,1,0:T(8,128)(2,1)}, bf16[4,8,64,128]{3,2,1,0:T(8,128)(2,1)S(1)}, u32[]{:S(2)}, u32[]{:S(2)}) collective-permute-start(bf16[4,8,64,128]{3,2,1,0:T(8,128)(2,1)} %collective-permute-done.19), channel_id=1, source_target_pairs={{0,4},{2,6},{4,0},{6,2},{8,12},{10,14},{12,8},{14,10},{16,20},{18,... | collective-permute-start | bytes 1572872 | tf_op jit(solution)/shard_map/ppermute | solution.py:45
  434.3 13.4 %collective-permute-start.21 = (bf16[4,8,64,128]{3,2,1,0:T(8,128)(2,1)S(1)}, bf16[4,8,64,128]{3,2,1,0:T(8,128)(2,1)S(1)}, u32[]{:S(2)}, u32[]{:S(2)}) collective-permute-start(bf16[4,8,64,128]{3,2,1,0:T(8,128)(2,1)S(1)} %collective-permute-done.20), channel_id=1, source_target_pairs={{0,8},{2,10},{4,12},{6,14},{8,0},{10,2},{12,4},{14,6},{16,24},{18,... | collective-permute-start | bytes 1572872 | tf_op jit(solution)/shard_map/ppermute | solution.py:45
  447.7 24.6 %collective-permute-start.22 = (bf16[4,8,64,128]{3,2,1,0:T(8,128)(2,1)S(1)}, bf16[4,8,64,128]{3,2,1,0:T(8,128)(2,1)S(1)}, u32[]{:S(2)}, u32[]{:S(2)}) collective-permute-start(bf16[4,8,64,128]{3,2,1,0:T(8,128)(2,1)S(1)} %collective-permute-done.21), channel_id=1, source_target_pairs={{0,16},{2,18},{4,20},{6,22},{8,24},{10,26},{12,28},{14,30},{16,0},... | collective-permute-start | bytes 1572872 | tf_op jit(solution)/shard_map/ppermute | solution.py:45
  449.0 24.3 %copy-start.2 = (f32[4,8,128,128]{3,2,1,0:T(8,128)S(1)}, f32[4,8,128,128]{3,2,1,0:T(8,128)}, u32[]{:S(2)}) copy-start(f32[4,8,128,128]{3,2,1,0:T(8,128)} %custom-call) | copy-start | bytes 6291460
  540.5 267.6 %all-reduce.3.cloned.1.call-start = ((), (), s32[]{:S(2)}) async-start(), calls=%async_computation.1 | async-start | bytes 2097152 | tf_op jit(solution)/shard_map/psum | solution.py:326
  541.0 26.8 %copy-start.11 = (f32[4,8,192,64]{3,2,1,0:T(8,128)S(1)}, f32[4,8,192,64]{3,2,1,0:T(8,128)}, u32[]{:S(2)}) copy-start(f32[4,8,192,64]{3,2,1,0:T(8,128)} %copy-done.10) | copy-start | bytes 4718596
  665.2 38.6 %copy-start.21 = (bf16[128,512]{0,1:T(8,128)(2,1)S(1)}, bf16[128,512]{0,1:T(8,128)(2,1)}, u32[]{:S(2)}) copy-start(bf16[128,512]{0,1:T(8,128)(2,1)} %copy-done.20) | copy-start | bytes 393220
  757.3 53.0 %copy-start.1 = (bf16[32,128,64]{1,2,0:T(8,128)(2,1)S(1)}, bf16[32,128,64]{1,2,0:T(8,128)(2,1)}, u32[]{:S(2)}) copy-start(bf16[32,128,64]{1,2,0:T(8,128)(2,1)} %param.21) | copy-start | bytes 1572868
  (33 other events, 162.0 us)
Sparse Core Ops, SparseCore 0:
  10.2 49.6 all-gather.7
  62.0 150.8 all-gather.9
  540.6 124.5 all-gather.11
  716.6 91.4 all-reduce.2
